TPU v7x, 256 devices: a whole 4x4x8 slice. The times are simulated.
256 devices in a mesh: loop: 128 (over y, z, x_hi, core), grp: 2 (over x_lo).
Axes of the slice: x: 4 (x_hi: 2, x_lo: 2; x = x_hi * 2 + x_lo), y: 4, z: 8, core: 2. Of those that a mesh axis runs over, the one named last changes fastest.
Arguments:
- jacobian: float32 [768, 16384], P('grp', 'loop'), may hold values from -0.21875 to 0.21875
Outputs:
- normal_matrix: float32 [16384, 16384], P(('loop', 'grp'))
All inputs are finite; a program needn't handle non-finite values.
Results may differ from a plain program's by a relative error of at most 0.00007.
Values sent between devices are 32-bit elements; how exact they have to be, the bound alone decides.
A program may use at most 128 MiB of HBM per device.

v0:
```python
import jax
import jax.numpy as jnp
from jax import lax
from jax.sharding import PartitionSpec as P

damping = 0.1


def gram_block(left_block, right_block):
    return lax.dot_general(
        left_block,
        right_block,
        (((0,), (0,)), ((), ())),
        precision=lax.Precision.HIGHEST,
        preferred_element_type=jnp.float32,
    )


def per_device(jacobian):
    partial_value = gram_block(jacobian, lax.all_gather(jacobian, "loop", axis=1, tiled=True))
    gram_rows = lax.psum_scatter(partial_value, "grp", scatter_dimension=0, tiled=True)
    row_count = gram_rows.shape[0]
    row_start = (lax.axis_index("loop") * lax.axis_size("grp") + lax.axis_index("grp")) * row_count
    row_ids = row_start + jnp.arange(row_count, dtype=jnp.int32)[:, None]
    col_ids = jnp.arange(gram_rows.shape[1], dtype=jnp.int32)[None, :]
    factor = jnp.where(row_ids == col_ids, jnp.float32(1.0 + damping), jnp.float32(1.0))
    return gram_rows * factor


def solution(mesh):
    in_specs = (P("grp", "loop"),)
    out_specs = P(("loop", "grp"), None)
    return jax.shard_map(
        per_device, mesh=mesh, in_specs=in_specs, out_specs=out_specs, check_vma=False
    )
```

profile of v0, /device:TPU:1, one launch (start us, length us, event | category | flops | bytes accessed | tf_op | source)
XLA Modules:
  0.0 338.0 jit_solution(15772389615527118351)
XLA Ops:
  6.5 0.0 all-gather.2.cloned.1.call-start
  6.5 0.7 all-gather.2.cloned.1.call-update
  7.3 0.0 reduce-scatter.2.cloned.1.call-start
  7.3 195.4 %all-gather.2.cloned.1.call-done = f32[384,16384]{1,0:T(8,128)} async-done(((f32[384,128]{1,0:T(8,128)}), f32[384,16384]{1,0:T(8,128)}) %all-gather.2.cloned.1.call-update) | async-done | bytes 25165840 | tf_op jit(solution)/shard_map/all_gather | solution.py:20
  202.7 23.3 %fusion = f32[128,16384]{1,0:T(8,128)} fusion(f32[384,128]{1,0:T(8,128)} %param.1, f32[384,16384]{1,0:T(8,128)} %all-gather.2.cloned.1.call-done), kind=kOutput, calls=%fused_computation.3 | convolution fusion | flops 9663676416 | bytes 33751040 | tf_op jit(solution)/shard_map/dot_general | solution.py:10
  226.0 0.0 reduce-scatter.2.cloned.1.call-update
  226.0 100.4 %reduce-scatter.2.cloned.1.call-done = f32[64,16384]{1,0:T(8,128)} async-done(((f32[128,16384]{1,0:T(8,128)}), f32[64,16384]{1,0:T(8,128)}) %reduce-scatter.2.cloned.1.call-update) | async-done | bytes 4194320 | tf_op jit(solution)/shard_map/reduce_scatter | solution.py:21
  326.5 4.7 %select_multiply_fusion = f32[64,16384]{1,0:T(8,128)} fusion(f32[64,16384]{1,0:T(8,128)} %reduce-scatter.2.cloned.1.call-done, s32[64]{0:T(128)S(1)} %iota_add_fusion), kind=kLoop, calls=%fused_computation | loop fusion | flops 3145728 | bytes 8388864 | tf_op jit(solution)/shard_map/mul | solution.py:27
  (1 shorter events, 0.0 us)
Async XLA Ops:
  6.5 196.2 %all-gather.2.cloned.1.call-start = ((), (), s32[]{:S(2)}) async-start(), calls=%async_computation.1 | async-start | bytes 25362432 | tf_op jit(solution)/shard_map/all_gather | solution.py:20
  7.3 319.2 %reduce-scatter.2.cloned.1.call-start = ((), (), s32[]{:S(2)}) async-start(), calls=%async_computation.2 | async-start | bytes 12582912 | tf_op jit(solution)/shard_map/reduce_scatter | solution.py:21
Sparse Core Ops, SparseCore 0:
  11.2 191.4 all-gather.1
  226.1 100.2 reduce-scatter.1
where the time goes:
time: 338 us
  waiting for transfers between devices  297 us (88%)
  matrix products  23.3 us (7%)
  between operations  13.4 us (4%)
  other arithmetic  4.72 us (1%)
    all_gather x1, waiting for transfers between devices, per_device(): lax.all_gather(jacobian, 'loop', axis=1, tiled=True)  195 us
    reduce_scatter x1, waiting for transfers between devices, per_device(): lax.psum_scatter(partial_value, 'grp', scatter_dimension=0, tiled=True)  100 us
    dot_general x1, matrix products, gram_block(): lax.dot_general(left_block, right_block, (((0,), (0,)), ((), ())), precis...  23.3 us
  transfers between devices with their start and end apart: 2, of which 2 were waited for; matrix products, arithmetic and copies ran while one was open for 0% of the time, Pallas kernels for 0%

commit v1 on v0

v1 whole, which is shorter than its diff:
```python
import jax
import jax.numpy as jnp
from jax import lax
from jax.experimental import pallas as pl
from jax.experimental.pallas import tpu as pltpu
from jax.sharding import PartitionSpec as P

damping = 0.1
MESH = pl.DeviceIdType.MESH
NX, NY, NZ, NC = 4, 4, 8, 2
DEPTH, WIDTH, OWN = 384, 128, 64
FIRST = 192


def kernel(
    a_ref,
    out_ref,
    turned,
    rows_f32,
    rows_high,
    rows_low,
    cols,
    prod,
    swap_s,
    swap_r,
    row_s,
    row_r,
    pass_s,
    pass_r,
    xf_s,
    xf_r,
    zl_s,
    zl_r,
    zs_s,
    zs_r,
    xb_s,
    xb_r,
    out_s,
    out_r,
):
    loop, xl = lax.axis_index("loop"), lax.axis_index("grp")
    c = loop % 2
    xh = (loop // 2) % 2
    z = (loop // 4) % NZ
    y = loop // 32
    x = xh * 2 + xl
    me = y * 2 + c
    way = 1 - 2 * c

    def device(dx=0, dy=0, dz=0, dc=0):
        xx, yy, zz, cc = (x + dx) % NX, (y + dy) % NY, (z + dz + NZ) % NZ, (c + dc) % NC
        return ((yy * NZ + zz) * 2 + xx // 2) * 2 + cc, xx % 2

    mate = (loop, 1 - xl)
    sends = []

    def send(src, dst, s_sem, r_sem, to):
        copy = pltpu.make_async_remote_copy(
            src_ref=src, dst_ref=dst, send_sem=s_sem, recv_sem=r_sem, device_id=to, device_id_type=MESH
        )
        copy.start()
        sends.append(copy)

    def arrived(ref, r_sem, s_sem):
        pltpu.make_async_remote_copy(
            src_ref=ref, dst_ref=ref, send_sem=s_sem, recv_sem=r_sem, device_id=mate, device_id_type=MESH
        ).wait_recv()

    def piece(dx, zz, start=0, size=DEPTH):
        xx = (x + dx) % NX
        return cols.at[zz, xx // 2, pl.ds(pl.multiple_of((xx % 2) * DEPTH + start, 8), size), :]

    def first(dx, zz):
        return piece(dx, zz, 0, FIRST)

    def rest(dx, zz):
        return piece(dx, zz, FIRST, DEPTH - FIRST)

    half = pl.ds(pl.multiple_of(xl * DEPTH, 128), DEPTH)
    other_half = pl.ds(pl.multiple_of((1 - xl) * DEPTH, 128), DEPTH)

    own = a_ref[...]
    cols[z, xh, pl.ds(pl.multiple_of(xl * DEPTH, 8), DEPTH), :] = own
    turned[...] = own.T
    rows_f32[me, :, half] = turned[pl.ds(pl.multiple_of(xl * OWN, 8), OWN), :]

    barrier = pltpu.get_barrier_semaphore()
    greeted = [device(dx=d) for d in (1, 2, 3)] + [device(dz=1), device(dz=-1), device(dc=1)]
    greeted += [device(dy=d, dc=e) for d in (1, 2, 3) for e in (0, 1)]
    for who in greeted:
        pl.semaphore_signal(barrier, inc=1, device_id=who, device_id_type=MESH)
    pl.semaphore_wait(barrier, len(greeted))

    send(
        turned.at[pl.ds(pl.multiple_of((1 - xl) * OWN, 8), OWN), :],
        rows_f32.at[me, :, half],
        swap_s.at[0],
        swap_r.at[0],
        mate,
    )
    up, down = device(dz=way), device(dz=-way)
    for t in (1, 3, 2):
        send(piece(0, z), piece(0, z), xf_s.at[4 - t - 1], xf_r.at[4 - t - 1], device(dx=t))
    send(piece(0, z), piece(0, z), zl_s.at[0, 0], zl_r.at[0, 0], up)
    send(piece(0, z), piece(0, z), zs_s.at[0, 0], zs_r.at[0, 0], down)

    arrived(rows_f32.at[me, :, other_half], swap_r.at[0], swap_s.at[0])
    for t in (1, 3, 2):
        send(rows_f32.at[me], rows_f32.at[me], row_s.at[4 - t - 1], row_r.at[4 - t - 1], device(dy=t))
    send(rows_f32.at[me], rows_f32.at[me], row_s.at[3], row_r.at[3], device(dc=1))

    for dx in (1, 3, 2):
        arrived(piece(dx, z), xf_r.at[dx - 1], xf_s.at[dx - 1])
        send(first(dx, z), first(dx, z), zl_s.at[0, dx], zl_r.at[0, dx], up)
        send(first(dx, z), first(dx, z), zs_s.at[0, dx], zs_r.at[0, dx], down)

    for dy in (1, 3, 2):
        slot = rows_f32.at[((y + dy) % NY) * 2 + c]
        arrived(slot, row_r.at[dy - 1], row_s.at[dy - 1])
        send(slot, slot, pass_s.at[dy - 1], pass_r.at[dy - 1], device(dc=1))
    arrived(rows_f32.at[y * 2 + 1 - c], row_r.at[3], row_s.at[3])
    for dy in (1, 3, 2):
        arrived(rows_f32.at[((y + dy) % NY) * 2 + 1 - c], pass_r.at[dy - 1], pass_s.at[dy - 1])

    rows = rows_f32[...].reshape(NY * NC * OWN, 2 * DEPTH)
    high = rows.astype(jnp.bfloat16)
    rows_high[...] = high
    rows_low[...] = (rows - high.astype(jnp.float32)).astype(jnp.bfloat16)

    def multiply(unit, zz):
        block = jnp.concatenate([cols[zz, 0], cols[zz, 1]], axis=1)
        block_high = block.astype(jnp.bfloat16)
        block_low = (block - block_high.astype(jnp.float32)).astype(jnp.bfloat16)
        value = jnp.dot(rows_high[...], block_high, preferred_element_type=jnp.float32)
        value += jnp.dot(rows_low[...], block_high, preferred_element_type=jnp.float32)
        value += jnp.dot(rows_high[...], block_low, preferred_element_type=jnp.float32)
        prod[unit, 0] = value[:, :WIDTH]
        prod[unit, 1] = value[:, WIDTH:]
        for dy, dc in ((1, 0), (1, 1), (3, 0), (3, 1), (2, 0), (2, 1), (0, 1)):
            to = ((y + dy) % NY) * 2 + (c + dc) % NC
            there = ((4 - dy) % 4) * 2 + dc - 1
            send(
                prod.at[unit, :, pl.ds(pl.multiple_of(to * OWN, 8), OWN), :],
                out_ref.at[y, zz, :, c],
                out_s.at[unit, there],
                out_r.at[unit, there],
                device(dy=dy, dc=dc),
            )
        mine = pl.ds(pl.multiple_of(me * OWN, 8), OWN)
        out_ref[y, zz, 0, c] = prod[unit, 0, mine, :]
        out_ref[y, zz, 1, c] = prod[unit, 1, mine, :]
        if unit == 0:
            row_ids = lax.broadcasted_iota(jnp.int32, (OWN, WIDTH), 0) + xl * OWN
            col_ids = lax.broadcasted_iota(jnp.int32, (OWN, WIDTH), 1)
            factor = jnp.where(row_ids == col_ids, jnp.float32(1.0 + damping), jnp.float32(1.0))
            out_ref[y, zz, xh, c] = prod[unit, xh, mine, :] * factor

    def spread(zz, index):
        for t in (1, 3, 2):
            send(rest(0, zz), rest(0, zz), xb_s.at[index, 4 - t - 1], xb_r.at[index, 4 - t - 1], device(dx=t))

    def spread_arrived(zz, index):
        for dx in (1, 3, 2):
            arrived(rest(dx, zz), xb_r.at[index, dx - 1], xb_s.at[index, dx - 1])

    origin = lambda d: (z + d * way + NZ) % NZ
    multiply(0, z)
    for d in range(1, 5):
        low, top = origin(-d), origin(d)
        arrived(piece(0, low), zl_r.at[d - 1, 0], zl_s.at[d - 1, 0])
        if d < 4:
            send(piece(0, low), piece(0, low), zl_s.at[d, 0], zl_r.at[d, 0], up)
        spread(low, d - 1)
        if d < 4:
            arrived(piece(0, top), zs_r.at[d - 1, 0], zs_s.at[d - 1, 0])
            if d < 3:
                send(piece(0, top), piece(0, top), zs_s.at[d, 0], zs_r.at[d, 0], down)
            spread(top, 3 + d)
        for dx in (1, 3, 2):
            arrived(first(dx, low), zl_r.at[d - 1, dx], zl_s.at[d - 1, dx])
            if d < 4:
                send(first(dx, low), first(dx, low), zl_s.at[d, dx], zl_r.at[d, dx], up)
                arrived(first(dx, top), zs_r.at[d - 1, dx], zs_s.at[d - 1, dx])
                if d < 3:
                    send(first(dx, top), first(dx, top), zs_s.at[d, dx], zs_r.at[d, dx], down)
        if d > 1:
            spread_arrived(origin(1 - d), d - 2)
            multiply(2 * d - 3, origin(1 - d))
            spread_arrived(origin(d - 1), 2 + d)
            multiply(2 * d - 2, origin(d - 1))
    spread_arrived(origin(-4), 3)
    multiply(7, origin(-4))

    for unit, d in enumerate((0, -1, 1, -2, 2, -3, 3, -4)):
        for dy, dc in ((1, 0), (1, 1), (3, 0), (3, 1), (2, 0), (2, 1), (0, 1)):
            index = dy * 2 + dc - 1
            src_c = (c + dc) % NC
            zz = (z + d * (1 - 2 * src_c) + NZ) % NZ
            arrived(out_ref.at[(y + dy) % NY, zz, :, src_c], out_r.at[unit, index], out_s.at[unit, index])
    for copy in sends:
        copy.wait_send()


def per_device(jacobian):
    dma = pltpu.SemaphoreType.DMA
    tiles = pl.pallas_call(
        kernel,
        name="gather_multiply_scatter",
        out_shape=jax.ShapeDtypeStruct((NY, NZ, 2, NC, OWN, WIDTH), jnp.float32),
        in_specs=[pl.BlockSpec(memory_space=pltpu.VMEM)],
        out_specs=pl.BlockSpec(memory_space=pltpu.VMEM),
        scratch_shapes=[
            pltpu.VMEM((WIDTH, DEPTH), jnp.float32),
            pltpu.VMEM((NY * NC, OWN, 2 * DEPTH), jnp.float32),
            pltpu.VMEM((NY * NC * OWN, 2 * DEPTH), jnp.bfloat16),
            pltpu.VMEM((NY * NC * OWN, 2 * DEPTH), jnp.bfloat16),
            pltpu.VMEM((NZ, 2, 2 * DEPTH, WIDTH), jnp.float32),
            pltpu.VMEM((NZ, 2, NY * NC * OWN, WIDTH), jnp.float32),
            dma((1,)),
            dma((1,)),
            dma((4,)),
            dma((4,)),
            dma((3,)),
            dma((3,)),
            dma((3,)),
            dma((3,)),
            dma((4, 4)),
            dma((4, 4)),
            dma((3, 4)),
            dma((3, 4)),
            dma((7, 3)),
            dma((7, 3)),
            dma((8, 7)),
            dma((8, 7)),
        ],
        compiler_params=pltpu.CompilerParams(
            collective_id=0, has_side_effects=True, vmem_limit_bytes=48 * 2**20
        ),
    )(jacobian)
    tiles = tiles.reshape(NY * NZ * 2 * NC, OWN, WIDTH)
    return jnp.transpose(tiles, (1, 0, 2)).reshape(OWN, NY * NZ * 2 * NC * WIDTH)


def solution(mesh):
    return jax.shard_map(
        per_device,
        mesh=mesh,
        in_specs=(P("grp", "loop"),),
        out_specs=P(("loop", "grp"), None),
        check_vma=False,
    )
```

time: 338 us -> 87.5 us (0.26)
  waiting for transfers between devices: 297 us -> 0 us
  Pallas kernels: 0 us -> 84.2 us
  matrix products: 23.3 us -> 0 us
  between operations: 13.4 us -> 0.01 us
  other arithmetic: 4.72 us -> 0 us
    all_gather x1 -> x0, waiting for transfers between devices: 195 us -> none  [per_device(): lax.all_gather(jacobian, 'loop', axis=1, tiled=True)]
    reduce_scatter x1 -> x0, waiting for transfers between devices: 100 us -> none  [per_device(): lax.psum_scatter(partial_value, 'grp', scatter_dimension=0, tiled=True)]
    pallas_call x0 -> x1, Pallas kernels: none -> 84.2 us  [per_device(): pl.pallas_call(kernel, name='gather_multiply_scatter', out_shape=jax.Shap...]
    dot_general x1 -> x0, matrix products: 23.3 us -> none  [gram_block(): lax.dot_general(left_block, right_block, (((0,), (0,)), ((), ())), precis...]
    mul x1 -> x0, other arithmetic: 4.72 us -> none  [per_device(): return gram_rows * factor]
  transfers between devices with their start and end apart: 2 -> 0, of which waited for: 2 -> 0; matrix products, arithmetic and copies ran while one was open for 0% -> 0% of each run, Pallas kernels for 0% -> 0%
where the time goes in v1:
time: 87.5 us; the launch traced here: 87.4 us
  Pallas kernels  84.2 us (96%)
  local copies, waits for them, and re-layouts  3.21 us (4%)
    pallas_call x1, Pallas kernels, per_device(): pl.pallas_call(kernel, name='gather_multiply_scatter', out_shape=jax.Shap...  84.2 us
    reshape x1, local copies, waits for them, and re-layouts, per_device(): jnp.transpose(tiles, (1, 0, 2)).reshape(OWN, NY * NZ * 2 * NC * WIDTH)  2.28 us

profile of v1, /device:TPU:1, one launch (start us, length us, event | category | flops | bytes accessed | tf_op | source)
XLA Modules:
  0.0 87.4 jit_solution(5027601112688478967)
XLA Ops:
  0.0 0.0 copy-start
  0.0 0.9 %copy-done = f32[384,128]{1,0:T(8,128)S(1)} copy-done((f32[384,128]{1,0:T(8,128)S(1)}, f32[384,128]{1,0:T(8,128)}, u32[]{:S(2)}) %copy-start) | copy-done | bytes 196632
  0.9 84.2 %gather_multiply_scatter.1 = f32[4,8,2,2,64,128]{5,4,3,2,1,0:T(8,128)S(1)} custom-call(f32[384,128]{1,0:T(8,128)S(1)} %copy-done), custom_call_target="tpu_custom_call" | custom-call | tf_op jit(solution)/shard_map/gather_multiply_scatter/pallas_call | solution.py:206
  85.1 2.3 %copy.5 = f32[128,8,8,128]{3,2,0,1:T(8,128)} copy(f32[128,8,8,128]{3,2,1,0:T(8,128)S(1)} %bitcast.7) | data formatting | bytes 8388608 | tf_op jit(solution)/shard_map/reshape | solution.py:241
Async XLA Ops:
  0.0 0.9 %copy-start = (f32[384,128]{1,0:T(8,128)S(1)}, f32[384,128]{1,0:T(8,128)}, u32[]{:S(2)}) copy-start(f32[384,128]{1,0:T(8,128)} %a_ref.1) | copy-start | bytes 589828

commit v2 on v1

v2 whole, which is shorter than its diff:
```python
import jax
import jax.numpy as jnp
from jax import lax
from jax.experimental import pallas as pl
from jax.experimental.pallas import tpu as pltpu
from jax.sharding import PartitionSpec as P

damping = 0.1
MESH = pl.DeviceIdType.MESH
NX, NY, NZ, NC = 4, 4, 8, 2
DEPTH, WIDTH, OWN = 384, 128, 64
FIRST = 152


SLOT = {(1, 0): 0, (3, 0): 1, (1, 1): 2, (3, 1): 3, (2, 0): 4, (2, 1): 5, (0, 0): 6, (0, 1): 7}


def kernel(
    a_ref,
    out_ref,
    own,
    turned,
    rows_f32,
    rows_high,
    rows_low,
    cols,
    prod,
    own_sem,
    swap_s,
    swap_r,
    row_s,
    row_r,
    pass_s,
    pass_r,
    xf_s,
    xf_r,
    zl_s,
    zl_r,
    zs_s,
    zs_r,
    xb_s,
    xb_r,
    out_s,
    out_r,
):
    loop, xl = lax.axis_index("loop"), lax.axis_index("grp")
    c = loop % 2
    xh = (loop // 2) % 2
    z = (loop // 4) % NZ
    y = loop // 32
    x = xh * 2 + xl
    way = 1 - 2 * c

    def device(dx=0, dy=0, dz=0, dc=0):
        xx, yy, zz = (x + dx * way + NX) % NX, (y + dy * way + NY) % NY, (z + dz * way + NZ) % NZ
        return ((yy * NZ + zz) * 2 + xx // 2) * 2 + (c + dc) % NC, xx % 2

    sends = []

    def send(src, dst, s_sem, r_sem, to):
        copy = pltpu.make_async_remote_copy(
            src_ref=src, dst_ref=dst, send_sem=s_sem, recv_sem=r_sem, device_id=to, device_id_type=MESH
        )
        copy.start()
        sends.append(copy)

    mate = (loop, 1 - xl)

    def arrived(ref, r_sem, s_sem):
        pltpu.make_async_remote_copy(
            src_ref=ref, dst_ref=ref, send_sem=s_sem, recv_sem=r_sem, device_id=mate, device_id_type=MESH
        ).wait_recv()

    def piece(dx, zz, start=0, size=DEPTH):
        xx = (x + dx * way + NX) % NX
        return cols.at[zz, xx // 2, pl.ds(pl.multiple_of((xx % 2) * DEPTH + start, 8), size), :]

    def first(dx, zz):
        return piece(dx, zz, 0, FIRST)

    def rest(dx, zz):
        return piece(dx, zz, FIRST, DEPTH - FIRST)

    def origin(d):
        return (z + d * way + NZ) % NZ

    half = pl.ds(pl.multiple_of(xl * DEPTH, 128), DEPTH)
    other_half = pl.ds(pl.multiple_of((1 - xl) * DEPTH, 128), DEPTH)

    load = pltpu.make_async_copy(a_ref, own, own_sem)
    load.start()
    barrier = pltpu.get_barrier_semaphore()
    greeted = [device(dx=d) for d in (1, 2, 3)] + [device(dz=1), device(dz=-1), device(dc=1)]
    greeted += [device(dy=d, dc=e) for d in (1, 2, 3) for e in (0, 1)]
    for who in greeted:
        pl.semaphore_signal(barrier, inc=1, device_id=who, device_id_type=MESH)
    load.wait()
    block = own[...]
    turned[...] = block.T
    rows_f32[SLOT[0, 0], :, half] = turned[pl.ds(pl.multiple_of(xl * OWN, 8), OWN), :]
    cols[z, xh, pl.ds(pl.multiple_of(xl * DEPTH, 8), DEPTH), :] = block
    pl.semaphore_wait(barrier, len(greeted))

    send(
        turned.at[pl.ds(pl.multiple_of((1 - xl) * OWN, 8), OWN), :],
        rows_f32.at[SLOT[0, 0], :, half],
        swap_s.at[0],
        swap_r.at[0],
        mate,
    )

    def give_rows(part, lanes):
        for to, there in ((1, 3), (-1, 1)):
            send(
                rows_f32.at[SLOT[0, 0], :, lanes],
                rows_f32.at[SLOT[there, 0], :, lanes],
                row_s.at[part, there - 1],
                row_r.at[part, there - 1],
                device(dy=to),
            )

    def rows_arrived(part, lanes, dy):
        slot = rows_f32.at[SLOT[dy, 0], :, lanes]
        arrived(slot, row_r.at[part, dy - 1], row_s.at[part, dy - 1])
        if dy == 3:
            send(slot, rows_f32.at[SLOT[2, 0], :, lanes], row_s.at[part, 1], row_r.at[part, 1], device(dy=1))

    def pass_rows(dy):
        send(
            rows_f32.at[SLOT[dy, 0]],
            rows_f32.at[SLOT[(4 - dy) % 4, 1]],
            pass_s.at[(4 - dy) % 4],
            pass_r.at[(4 - dy) % 4],
            device(dc=1),
        )

    def passed(dy):
        arrived(rows_f32.at[SLOT[dy, 1]], pass_r.at[dy], pass_s.at[dy])

    give_rows(0, half)
    towards = (1 - 2 * xl) * way
    for to in (towards, -towards):
        send(piece(0, z), piece(0, z), xf_s.at[1 + to], xf_r.at[1 + to], device(dx=to))
    up, down = device(dz=1), device(dz=-1)
    send(piece(0, z), piece(0, z), zl_s.at[0, 0], zl_r.at[0, 0], up)
    send(piece(0, z), piece(0, z), zs_s.at[0, 0], zs_r.at[0, 0], down)

    arrived(rows_f32.at[SLOT[0, 0], :, other_half], swap_r.at[0], swap_s.at[0])
    give_rows(1, other_half)
    pass_rows(0)
    rows_arrived(0, half, 3)
    rows_arrived(0, half, 1)
    rows_arrived(1, other_half, 3)
    pass_rows(3)
    rows_arrived(1, other_half, 1)
    pass_rows(1)

    def ring_start(dx):
        send(first(dx, z), first(dx, z), zl_s.at[0, dx], zl_r.at[0, dx], up)
        send(first(dx, z), first(dx, z), zs_s.at[0, dx], zs_r.at[0, dx], down)

    arrived(piece(3, z), xf_r.at[2], xf_s.at[2])
    send(piece(3, z), piece(3, z), xf_s.at[1], xf_r.at[1], device(dx=1))
    ring_start(3)
    arrived(piece(1, z), xf_r.at[0], xf_s.at[0])
    ring_start(1)

    def split(slots):
        part = pl.ds(slots.start * OWN, (slots.stop - slots.start) * OWN)
        rows = rows_f32[slots].reshape((slots.stop - slots.start) * OWN, 2 * DEPTH)
        high = rows.astype(jnp.bfloat16)
        rows_high[part, :] = high
        rows_low[part, :] = (rows - high.astype(jnp.float32)).astype(jnp.bfloat16)

    def product(part, block):
        block_high = block.astype(jnp.bfloat16)
        block_low = (block - block_high.astype(jnp.float32)).astype(jnp.bfloat16)
        value = jnp.dot(rows_high[part, :], block_high, preferred_element_type=jnp.float32)
        value += jnp.dot(rows_low[part, :], block_high, preferred_element_type=jnp.float32)
        value += jnp.dot(rows_high[part, :], block_low, preferred_element_type=jnp.float32)
        return value

    def deliver(group, src, dst, who):
        for dy, dc in who:
            there = (4 - dy) % 4 if dc == 0 else dy
            index = there * 2 + dc - 1
            k = SLOT[dy, dc]
            send(src(pl.ds(k * OWN, OWN)), dst, out_s.at[group, index], out_r.at[group, index], device(dy=dy, dc=dc))

    NEAR, FAR = ((1, 0), (3, 0), (1, 1), (3, 1)), ((2, 0), (2, 1), (0, 1))
    mine = pl.ds(SLOT[0, 0] * OWN, OWN)

    def own_plane(group, hh, part, who):
        prod[0, hh, part, :] = product(part, cols[z, hh])
        deliver(group, lambda r: prod.at[0, hh, r, :], out_ref.at[y, z, hh, c], who)

    near_rows, far_rows = pl.ds(0, 4 * OWN), pl.ds(4 * OWN, 4 * OWN)
    passed(1)
    passed(3)
    split(slice(0, 4))
    own_plane(0, xh, near_rows, NEAR)
    for part, lanes in ((0, half), (1, other_half)):
        rows_arrived(part, lanes, 2)
    pass_rows(2)
    arrived(piece(2, z), xf_r.at[1], xf_s.at[1])
    ring_start(2)
    passed(0)
    own_plane(8, 1 - xh, near_rows, NEAR)
    passed(2)
    split(slice(4, 8))
    own_plane(0, xh, far_rows, FAR)
    row_ids = lax.broadcasted_iota(jnp.int32, (OWN, WIDTH), 0) + xl * OWN
    col_ids = lax.broadcasted_iota(jnp.int32, (OWN, WIDTH), 1)
    factor = jnp.where(row_ids == col_ids, jnp.float32(1.0 + damping), jnp.float32(1.0))
    out_ref[y, z, xh, c] = prod[0, xh, mine, :] * factor
    own_plane(8, 1 - xh, far_rows, FAR)
    out_ref[y, z, 1 - xh, c] = prod[0, 1 - xh, mine, :]

    def multiply(unit, zz):
        value = product(pl.ds(0, 8 * OWN), jnp.concatenate([cols[zz, 0], cols[zz, 1]], axis=1))
        prod[unit, 0] = value[:, :WIDTH]
        prod[unit, 1] = value[:, WIDTH:]
        deliver(unit, lambda r: prod.at[unit, :, r, :], out_ref.at[y, zz, :, c], NEAR + FAR)
        out_ref[y, zz, 0, c] = prod[unit, 0, mine, :]
        out_ref[y, zz, 1, c] = prod[unit, 1, mine, :]

    def spread(zz, index):
        for to, there in ((1, 3), (-1, 1)):
            send(rest(0, zz), rest(0, zz), xb_s.at[index, there - 1], xb_r.at[index, there - 1], device(dx=to))

    def spread_on(zz, index):
        arrived(rest(3, zz), xb_r.at[index, 2], xb_s.at[index, 2])
        send(rest(3, zz), rest(3, zz), xb_s.at[index, 1], xb_r.at[index, 1], device(dx=1))

    def spread_done(zz, index):
        for dx in (1, 2):
            arrived(rest(dx, zz), xb_r.at[index, dx - 1], xb_s.at[index, dx - 1])

    for d in range(1, 5):
        low, top = origin(-d), origin(d)
        arrived(piece(0, low), zl_r.at[d - 1, 0], zl_s.at[d - 1, 0])
        if d < 4:
            send(piece(0, low), piece(0, low), zl_s.at[d, 0], zl_r.at[d, 0], up)
        spread(low, d - 1)
        if d < 4:
            arrived(piece(0, top), zs_r.at[d - 1, 0], zs_s.at[d - 1, 0])
            if d < 3:
                send(piece(0, top), piece(0, top), zs_s.at[d, 0], zs_r.at[d, 0], down)
            spread(top, 3 + d)
        for dx in (3, 1, 2):
            arrived(first(dx, low), zl_r.at[d - 1, dx], zl_s.at[d - 1, dx])
            if d < 4:
                send(first(dx, low), first(dx, low), zl_s.at[d, dx], zl_r.at[d, dx], up)
                arrived(first(dx, top), zs_r.at[d - 1, dx], zs_s.at[d - 1, dx])
                if d < 3:
                    send(first(dx, top), first(dx, top), zs_s.at[d, dx], zs_r.at[d, dx], down)
        spread_on(low, d - 1)
        if d < 4:
            spread_on(top, 3 + d)
        if d > 1:
            spread_done(origin(1 - d), d - 2)
            multiply(2 * d - 3, origin(1 - d))
            spread_done(origin(d - 1), 2 + d)
            multiply(2 * d - 2, origin(d - 1))
    spread_done(origin(-4), 3)
    multiply(7, origin(-4))

    for dy, dc in NEAR + FAR:
        index = dy * 2 + dc - 1
        yy, cc = (y + dy * way + NY) % NY, (c + dc) % NC
        for group, hh in ((0, xh), (8, 1 - xh)):
            arrived(out_ref.at[yy, z, hh, cc], out_r.at[group, index], out_s.at[group, index])
        for unit, d in enumerate((-1, 1, -2, 2, -3, 3, -4)):
            zz = (z + d * (1 - 2 * cc) + NZ) % NZ
            arrived(out_ref.at[yy, zz, :, cc], out_r.at[unit + 1, index], out_s.at[unit + 1, index])
    for copy in sends:
        copy.wait_send()


def per_device(jacobian):
    dma = pltpu.SemaphoreType.DMA
    tiles = pl.pallas_call(
        kernel,
        name="gather_multiply_scatter",
        out_shape=jax.ShapeDtypeStruct((NY, NZ, 2, NC, OWN, WIDTH), jnp.float32),
        in_specs=[pl.BlockSpec(memory_space=pltpu.HBM)],
        out_specs=pl.BlockSpec(memory_space=pltpu.VMEM),
        scratch_shapes=[
            pltpu.VMEM((DEPTH, WIDTH), jnp.float32),
            pltpu.VMEM((WIDTH, DEPTH), jnp.float32),
            pltpu.VMEM((NY * NC, OWN, 2 * DEPTH), jnp.float32),
            pltpu.VMEM((NY * NC * OWN, 2 * DEPTH), jnp.bfloat16),
            pltpu.VMEM((NY * NC * OWN, 2 * DEPTH), jnp.bfloat16),
            pltpu.VMEM((NZ, 2, 2 * DEPTH, WIDTH), jnp.float32),
            pltpu.VMEM((NZ, 2, NY * NC * OWN, WIDTH), jnp.float32),
            dma,
            dma((1,)),
            dma((1,)),
            dma((2, 3)),
            dma((2, 3)),
            dma((4,)),
            dma((4,)),
            dma((3,)),
            dma((3,)),
            dma((4, 4)),
            dma((4, 4)),
            dma((3, 4)),
            dma((3, 4)),
            dma((7, 3)),
            dma((7, 3)),
            dma((9, 7)),
            dma((9, 7)),
        ],
        compiler_params=pltpu.CompilerParams(
            collective_id=0, has_side_effects=True, vmem_limit_bytes=48 * 2**20
        ),
    )(jacobian)
    tiles = tiles.reshape(NY * NZ * 2 * NC, OWN, WIDTH)
    return jnp.transpose(tiles, (1, 0, 2)).reshape(OWN, NY * NZ * 2 * NC * WIDTH)


def solution(mesh):
    return jax.shard_map(
        per_device,
        mesh=mesh,
        in_specs=(P("grp", "loop"),),
        out_specs=P(("loop", "grp"), None),
        check_vma=False,
    )
```

time: 87.5 us -> 86.6 us (0.990)
  Pallas kernels: 84.2 us -> 82.6 us
    pallas_call x1, Pallas kernels: 84.2 us -> 82.6 us  [per_device(): pl.pallas_call(kernel, name='gather_multiply_scatter', out_shape=jax.Shap...]
where the time goes in v2:
time: 86.6 us; the launch traced here: 85.8 us
  Pallas kernels  82.6 us (95%)
  local copies, waits for them, and re-layouts  3.21 us (4%)
    pallas_call x1, Pallas kernels, per_device(): pl.pallas_call(kernel, name='gather_multiply_scatter', out_shape=jax.Shap...  82.6 us
    reshape x1, local copies, waits for them, and re-layouts, per_device(): jnp.transpose(tiles, (1, 0, 2)).reshape(OWN, NY * NZ * 2 * NC * WIDTH)  2.28 us

profile of v2, /device:TPU:1, one launch (start us, length us, event | category | flops | bytes accessed | tf_op | source)
XLA Modules:
  0.0 85.8 jit_solution(7295375817462982897)
XLA Ops:
  0.0 0.0 copy-start
  0.0 0.9 %copy-done = f32[384,128]{1,0:T(8,128)S(1)} copy-done((f32[384,128]{1,0:T(8,128)S(1)}, f32[384,128]{1,0:T(8,128)}, u32[]{:S(2)}) %copy-start) | copy-done | bytes 196632
  0.9 82.6 %gather_multiply_scatter.1 = f32[4,8,2,2,64,128]{5,4,3,2,1,0:T(8,128)S(1)} custom-call(f32[384,128]{1,0:T(8,128)S(1)} %copy-done), custom_call_target="tpu_custom_call" | custom-call | tf_op jit(solution)/shard_map/gather_multiply_scatter/pallas_call | solution.py:282
  83.6 2.3 %copy.5 = f32[128,8,8,128]{3,2,0,1:T(8,128)} copy(f32[128,8,8,128]{3,2,1,0:T(8,128)S(1)} %bitcast.7) | data formatting | bytes 8388608 | tf_op jit(solution)/shard_map/reshape | solution.py:319
Async XLA Ops:
  0.0 0.9 %copy-start = (f32[384,128]{1,0:T(8,128)S(1)}, f32[384,128]{1,0:T(8,128)}, u32[]{:S(2)}) copy-start(f32[384,128]{1,0:T(8,128)} %a_ref.1) | copy-start | bytes 589828

commit v3 on v2

--- a/solution.py
+++ b/solution.py
@@ -9,10 +9,92 @@
 MESH = pl.DeviceIdType.MESH
 NX, NY, NZ, NC = 4, 4, 8, 2
 DEPTH, WIDTH, OWN = 384, 128, 64
-FIRST = 152
+FIRST = 176
 
 
 SLOT = {(1, 0): 0, (3, 0): 1, (1, 1): 2, (3, 1): 3, (2, 0): 4, (2, 1): 5, (0, 0): 6, (0, 1): 7}
+NEAR, FAR = ((1, 0), (3, 0), (1, 1), (3, 1)), ((2, 0), (2, 1), (0, 1))
+UNITS = (-1, 1, -2, 2, -3, 3, -4)
+DIRECT = (-1, 1, -2, 2)
+ORDER = (
+    ("swap",),
+    ("rows", 0, 3),
+    ("first", "across"),
+    ("rows", 0, 1),
+    ("up", 1, "own"),
+    ("passed", 0),
+    ("first", "beyond"),
+    ("rows", 1, 3),
+    ("rows", 1, 1),
+    ("down", 1, "own"),
+    ("passed", 1),
+    ("first", "opposite"),
+    ("rows", 0, 2),
+    ("up", 1, "across"),
+    ("rest", "across"),
+    ("passed", 3),
+    ("near", 0),
+    ("rows", 1, 2),
+    ("down", 1, "across"),
+    ("rest", "beyond"),
+    ("passed", 2),
+    ("far", 0),
+    ("up", 2, "own"),
+    ("up", 1, "beyond"),
+    ("rest", "opposite"),
+    ("near", 8),
+    ("spread", -1, 3),
+    ("far", 8),
+    ("down", 1, "beyond"),
+    ("spread", -1, 1),
+    ("down", 2, "own"),
+    ("up", 1, "opposite"),
+    ("spread", -1, 2),
+    ("multiply", -1),
+    ("down", 1, "opposite"),
+    ("spread", 1, 3),
+    ("up", 2, "across"),
+    ("spread", 1, 1),
+    ("down", 2, "across"),
+    ("up", 3, "own"),
+    ("spread", 1, 2),
+    ("multiply", 1),
+    ("spread", -2, 3),
+    ("up", 2, "beyond"),
+    ("down", 2, "beyond"),
+    ("spread", -2, 1),
+    ("down", 3, "own"),
+    ("spread", -2, 2),
+    ("up", 2, "opposite"),
+    ("multiply", -2),
+    ("spread", 2, 3),
+    ("down", 2, "opposite"),
+    ("spread", 2, 1),
+    ("up", 3, "across"),
+    ("down", 3, "across"),
+    ("spread", 2, 2),
+    ("multiply", 2),
+    ("spread", -3, 3),
+    ("up", 4, "own"),
+    ("up", 3, "beyond"),
+    ("spread", -3, 1),
+    ("down", 3, "beyond"),
+    ("spread", 3, 3),
+    ("up", 3, "opposite"),
+    ("spread", 3, 1),
+    ("down", 3, "opposite"),
+    ("spread", -3, 2),
+    ("multiply", -3),
+    ("up", 4, "across"),
+    ("spread", -4, 3),
+    ("up", 4, "beyond"),
+    ("up", 4, "opposite"),
+    ("spread", -4, 1),
+    ("spread", 3, 2),
+    ("multiply", 3),
+    ("spread", -4, 2),
+    ("multiply", -4),
+)
 
 
 def kernel(
@@ -32,6 +114,8 @@
     row_r,
     pass_s,
     pass_r,
+    xa_s,
+    xa_r,
     xf_s,
     xf_r,
     zl_s,
@@ -137,33 +221,11 @@
     def passed(dy):
         arrived(rows_f32.at[SLOT[dy, 1]], pass_r.at[dy], pass_s.at[dy])
 
-    give_rows(0, half)
     towards = (1 - 2 * xl) * way
-    for to in (towards, -towards):
-        send(piece(0, z), piece(0, z), xf_s.at[1 + to], xf_r.at[1 + to], device(dx=to))
+    across, beyond = (towards + NX) % NX, (NX - towards) % NX
     up, down = device(dz=1), device(dz=-1)
-    send(piece(0, z), piece(0, z), zl_s.at[0, 0], zl_r.at[0, 0], up)
-    send(piece(0, z), piece(0, z), zs_s.at[0, 0], zs_r.at[0, 0], down)
-
-    arrived(rows_f32.at[SLOT[0, 0], :, other_half], swap_r.at[0], swap_s.at[0])
-    give_rows(1, other_half)
-    pass_rows(0)
-    rows_arrived(0, half, 3)
-    rows_arrived(0, half, 1)
-    rows_arrived(1, other_half, 3)
-    pass_rows(3)
-    rows_arrived(1, other_half, 1)
-    pass_rows(1)
-
-    def ring_start(dx):
-        send(first(dx, z), first(dx, z), zl_s.at[0, dx], zl_r.at[0, dx], up)
-        send(first(dx, z), first(dx, z), zs_s.at[0, dx], zs_r.at[0, dx], down)
-
-    arrived(piece(3, z), xf_r.at[2], xf_s.at[2])
-    send(piece(3, z), piece(3, z), xf_s.at[1], xf_r.at[1], device(dx=1))
-    ring_start(3)
-    arrived(piece(1, z), xf_r.at[0], xf_s.at[0])
-    ring_start(1)
+    near_rows, far_rows = pl.ds(0, 4 * OWN), pl.ds(4 * OWN, 4 * OWN)
+    mine = pl.ds(SLOT[0, 0] * OWN, OWN)
 
     def split(slots):
         part = pl.ds(slots.start * OWN, (slots.stop - slots.start) * OWN)
@@ -187,36 +249,29 @@
             k = SLOT[dy, dc]
             send(src(pl.ds(k * OWN, OWN)), dst, out_s.at[group, index], out_r.at[group, index], device(dy=dy, dc=dc))
 
-    NEAR, FAR = ((1, 0), (3, 0), (1, 1), (3, 1)), ((2, 0), (2, 1), (0, 1))
-    mine = pl.ds(SLOT[0, 0] * OWN, OWN)
-
     def own_plane(group, hh, part, who):
         prod[0, hh, part, :] = product(part, cols[z, hh])
         deliver(group, lambda r: prod.at[0, hh, r, :], out_ref.at[y, z, hh, c], who)
 
-    near_rows, far_rows = pl.ds(0, 4 * OWN), pl.ds(4 * OWN, 4 * OWN)
-    passed(1)
-    passed(3)
-    split(slice(0, 4))
-    own_plane(0, xh, near_rows, NEAR)
-    for part, lanes in ((0, half), (1, other_half)):
-        rows_arrived(part, lanes, 2)
-    pass_rows(2)
-    arrived(piece(2, z), xf_r.at[1], xf_s.at[1])
-    ring_start(2)
-    passed(0)
-    own_plane(8, 1 - xh, near_rows, NEAR)
-    passed(2)
-    split(slice(4, 8))
-    own_plane(0, xh, far_rows, FAR)
-    row_ids = lax.broadcasted_iota(jnp.int32, (OWN, WIDTH), 0) + xl * OWN
-    col_ids = lax.broadcasted_iota(jnp.int32, (OWN, WIDTH), 1)
-    factor = jnp.where(row_ids == col_ids, jnp.float32(1.0 + damping), jnp.float32(1.0))
-    out_ref[y, z, xh, c] = prod[0, xh, mine, :] * factor
-    own_plane(8, 1 - xh, far_rows, FAR)
-    out_ref[y, z, 1 - xh, c] = prod[0, 1 - xh, mine, :]
-
-    def multiply(unit, zz):
+    def plane_near(group, hh):
+        if group == 0:
+            split(slice(0, 4))
+        own_plane(group, hh, near_rows, NEAR)
+
+    def plane_far(group, hh):
+        if group == 0:
+            split(slice(4, 8))
+        own_plane(group, hh, far_rows, FAR)
+        if group == 0:
+            row_ids = lax.broadcasted_iota(jnp.int32, (OWN, WIDTH), 0) + xl * OWN
+            col_ids = lax.broadcasted_iota(jnp.int32, (OWN, WIDTH), 1)
+            factor = jnp.where(row_ids == col_ids, jnp.float32(1.0 + damping), jnp.float32(1.0))
+            out_ref[y, z, hh, c] = prod[0, hh, mine, :] * factor
+        else:
+            out_ref[y, z, hh, c] = prod[0, hh, mine, :]
+
+    def multiply(d):
+        unit, zz = UNITS.index(d) + 1, origin(d)
         value = product(pl.ds(0, 8 * OWN), jnp.concatenate([cols[zz, 0], cols[zz, 1]], axis=1))
         prod[unit, 0] = value[:, :WIDTH]
         prod[unit, 1] = value[:, WIDTH:]
@@ -224,53 +279,82 @@
         out_ref[y, zz, 0, c] = prod[unit, 0, mine, :]
         out_ref[y, zz, 1, c] = prod[unit, 1, mine, :]
 
-    def spread(zz, index):
+    def ring_start(dx, part):
+        send(part, part, zl_s.at[0, dx], zl_r.at[0, dx], up)
+        send(part, part, zs_s.at[0, dx], zs_r.at[0, dx], down)
+
+    def ring_up(d, dx):
+        part = piece(0, origin(-d)) if isinstance(dx, int) and dx == 0 else first(dx, origin(-d))
+        arrived(part, zl_r.at[d - 1, dx], zl_s.at[d - 1, dx])
+        if d < 4:
+            send(part, part, zl_s.at[d, dx], zl_r.at[d, dx], up)
+
+    def ring_down(d, dx):
+        part = piece(0, origin(d)) if isinstance(dx, int) and dx == 0 else first(dx, origin(d))
+        arrived(part, zs_r.at[d - 1, dx], zs_s.at[d - 1, dx])
+        if d < 3:
+            send(part, part, zs_s.at[d, dx], zs_r.at[d, dx], down)
+
+    def spread(d):
+        part, unit = rest(0, origin(d)), UNITS.index(d)
         for to, there in ((1, 3), (-1, 1)):
-            send(rest(0, zz), rest(0, zz), xb_s.at[index, there - 1], xb_r.at[index, there - 1], device(dx=to))
-
-    def spread_on(zz, index):
-        arrived(rest(3, zz), xb_r.at[index, 2], xb_s.at[index, 2])
-        send(rest(3, zz), rest(3, zz), xb_s.at[index, 1], xb_r.at[index, 1], device(dx=1))
-
-    def spread_done(zz, index):
-        for dx in (1, 2):
-            arrived(rest(dx, zz), xb_r.at[index, dx - 1], xb_s.at[index, dx - 1])
-
-    for d in range(1, 5):
-        low, top = origin(-d), origin(d)
-        arrived(piece(0, low), zl_r.at[d - 1, 0], zl_s.at[d - 1, 0])
-        if d < 4:
-            send(piece(0, low), piece(0, low), zl_s.at[d, 0], zl_r.at[d, 0], up)
-        spread(low, d - 1)
-        if d < 4:
-            arrived(piece(0, top), zs_r.at[d - 1, 0], zs_s.at[d - 1, 0])
-            if d < 3:
-                send(piece(0, top), piece(0, top), zs_s.at[d, 0], zs_r.at[d, 0], down)
-            spread(top, 3 + d)
-        for dx in (3, 1, 2):
-            arrived(first(dx, low), zl_r.at[d - 1, dx], zl_s.at[d - 1, dx])
-            if d < 4:
-                send(first(dx, low), first(dx, low), zl_s.at[d, dx], zl_r.at[d, dx], up)
-                arrived(first(dx, top), zs_r.at[d - 1, dx], zs_s.at[d - 1, dx])
-                if d < 3:
-                    send(first(dx, top), first(dx, top), zs_s.at[d, dx], zs_r.at[d, dx], down)
-        spread_on(low, d - 1)
-        if d < 4:
-            spread_on(top, 3 + d)
-        if d > 1:
-            spread_done(origin(1 - d), d - 2)
-            multiply(2 * d - 3, origin(1 - d))
-            spread_done(origin(d - 1), 2 + d)
-            multiply(2 * d - 2, origin(d - 1))
-    spread_done(origin(-4), 3)
-    multiply(7, origin(-4))
+            send(part, part, xb_s.at[unit, there - 1], xb_r.at[unit, there - 1], device(dx=to))
+        if d in DIRECT:
+            send(part, part, xb_s.at[unit, 1], xb_r.at[unit, 1], device(dx=2))
+
+    def spread_came(d, dx):
+        part, unit = rest(dx, origin(d)), UNITS.index(d)
+        arrived(part, xb_r.at[unit, dx - 1], xb_s.at[unit, dx - 1])
+        if dx == 3 and d not in DIRECT:
+            send(part, part, xb_s.at[unit, 1], xb_r.at[unit, 1], device(dx=1))
+
+    give_rows(0, half)
+    for part, s_sem, r_sem in ((first(0, z), xa_s, xa_r), (rest(0, z), xf_s, xf_r)):
+        send(part, part, s_sem.at[1 + towards], r_sem.at[1 + towards], device(dx=towards))
+        if s_sem is xa_s:
+            ring_start(0, piece(0, z))
+        send(part, part, s_sem.at[1 - towards], r_sem.at[1 - towards], device(dx=-towards))
+        send(part, part, s_sem.at[1], r_sem.at[1], device(dx=2))
+
+    for event in ORDER:
+        kind, at = event[0], event[1:]
+        if kind == "swap":
+            arrived(rows_f32.at[SLOT[0, 0], :, other_half], swap_r.at[0], swap_s.at[0])
+            give_rows(1, other_half)
+            pass_rows(0)
+        elif kind == "rows":
+            rows_arrived(at[0], (half, other_half)[at[0]], at[1])
+            if at[0] == 1:
+                pass_rows(at[1])
+        elif kind == "passed":
+            passed(at[0])
+        elif kind in ("first", "rest"):
+            dx = {"across": across, "beyond": beyond, "opposite": 2}[at[0]]
+            if kind == "first":
+                arrived(first(dx, z), xa_r.at[dx - 1], xa_s.at[dx - 1])
+                ring_start(dx, first(dx, z))
+            else:
+                arrived(rest(dx, z), xf_r.at[dx - 1], xf_s.at[dx - 1])
+        elif kind in ("up", "down"):
+            dx = {"own": 0, "across": across, "beyond": beyond, "opposite": 2}[at[1]]
+            (ring_up if kind == "up" else ring_down)(at[0], dx)
+            if at[1] == "own":
+                spread(-at[0] if kind == "up" else at[0])
+        elif kind == "spread":
+            spread_came(at[0], at[1])
+        elif kind == "near":
+            plane_near(at[0], xh if at[0] == 0 else 1 - xh)
+        elif kind == "far":
+            plane_far(at[0], xh if at[0] == 0 else 1 - xh)
+        else:
+            multiply(at[0])
 
     for dy, dc in NEAR + FAR:
         index = dy * 2 + dc - 1
         yy, cc = (y + dy * way + NY) % NY, (c + dc) % NC
         for group, hh in ((0, xh), (8, 1 - xh)):
             arrived(out_ref.at[yy, z, hh, cc], out_r.at[group, index], out_s.at[group, index])
-        for unit, d in enumerate((-1, 1, -2, 2, -3, 3, -4)):
+        for unit, d in enumerate(UNITS):
             zz = (z + d * (1 - 2 * cc) + NZ) % NZ
             arrived(out_ref.at[yy, zz, :, cc], out_r.at[unit + 1, index], out_s.at[unit + 1, index])
     for copy in sends:
@@ -302,6 +386,8 @@
             dma((4,)),
             dma((3,)),
             dma((3,)),
+            dma((3,)),
+            dma((3,)),
             dma((4, 4)),
             dma((4, 4)),
             dma((3, 4)),

time: 86.6 us -> 75.8 us (0.88)
  Pallas kernels: 82.6 us -> 72.5 us
    pallas_call x1, Pallas kernels: 82.6 us -> 72.5 us  [per_device(): pl.pallas_call(kernel, name='gather_multiply_scatter', out_shape=jax.Shap...]
where the time goes in v3:
time: 75.8 us; the launch traced here: 75.7 us
  Pallas kernels  72.5 us (96%)
  local copies, waits for them, and re-layouts  3.21 us (4%)
    pallas_call x1, Pallas kernels, per_device(): pl.pallas_call(kernel, name='gather_multiply_scatter', out_shape=jax.Shap...  72.5 us
    reshape x1, local copies, waits for them, and re-layouts, per_device(): jnp.transpose(tiles, (1, 0, 2)).reshape(OWN, NY * NZ * 2 * NC * WIDTH)  2.28 us

profile of v3, /device:TPU:1, one launch (start us, length us, event | category | flops | bytes accessed | tf_op | source)
XLA Modules:
  0.0 75.7 jit_solution(10667059373617560235)
XLA Ops:
  0.0 0.0 copy-start
  0.0 0.9 %copy-done = f32[384,128]{1,0:T(8,128)S(1)} copy-done((f32[384,128]{1,0:T(8,128)S(1)}, f32[384,128]{1,0:T(8,128)}, u32[]{:S(2)}) %copy-start) | copy-done | bytes 196632
  0.9 72.5 %gather_multiply_scatter.1 = f32[4,8,2,2,64,128]{5,4,3,2,1,0:T(8,128)S(1)} custom-call(f32[384,128]{1,0:T(8,128)S(1)} %copy-done), custom_call_target="tpu_custom_call" | custom-call | tf_op jit(solution)/shard_map/gather_multiply_scatter/pallas_call | solution.py:366
  73.4 2.3 %copy.5 = f32[128,8,8,128]{3,2,0,1:T(8,128)} copy(f32[128,8,8,128]{3,2,1,0:T(8,128)S(1)} %bitcast.7) | data formatting | bytes 8388608 | tf_op jit(solution)/shard_map/reshape | solution.py:405
Async XLA Ops:
  0.0 0.9 %copy-start = (f32[384,128]{1,0:T(8,128)S(1)}, f32[384,128]{1,0:T(8,128)}, u32[]{:S(2)}) copy-start(f32[384,128]{1,0:T(8,128)} %a_ref.1) | copy-start | bytes 589828

commit v4 on v3

--- a/solution.py
+++ b/solution.py
@@ -9,6 +9,7 @@
 MESH = pl.DeviceIdType.MESH
 NX, NY, NZ, NC = 4, 4, 8, 2
 DEPTH, WIDTH, OWN = 384, 128, 64
+TILES = OWN // 8
 FIRST = 176
 
 
@@ -225,7 +226,14 @@
     across, beyond = (towards + NX) % NX, (NX - towards) % NX
     up, down = device(dz=1), device(dz=-1)
     near_rows, far_rows = pl.ds(0, 4 * OWN), pl.ds(4 * OWN, 4 * OWN)
-    mine = pl.ds(SLOT[0, 0] * OWN, OWN)
+    mine = pl.ds(SLOT[0, 0] * TILES, TILES)
+
+    def part_tiles(part):
+        return pl.ds(part.start // 8, part.size // 8)
+
+    def tiles_of(value):
+        return value.reshape(value.shape[0] // 8, 8, WIDTH)
+
 
     def split(slots):
         part = pl.ds(slots.start * OWN, (slots.stop - slots.start) * OWN)
@@ -247,11 +255,11 @@
             there = (4 - dy) % 4 if dc == 0 else dy
             index = there * 2 + dc - 1
             k = SLOT[dy, dc]
-            send(src(pl.ds(k * OWN, OWN)), dst, out_s.at[group, index], out_r.at[group, index], device(dy=dy, dc=dc))
+            send(src(pl.ds(k * TILES, TILES)), dst, out_s.at[group, index], out_r.at[group, index], device(dy=dy, dc=dc))
 
     def own_plane(group, hh, part, who):
-        prod[0, hh, part, :] = product(part, cols[z, hh])
-        deliver(group, lambda r: prod.at[0, hh, r, :], out_ref.at[y, z, hh, c], who)
+        prod[0, part_tiles(part), hh] = tiles_of(product(part, cols[z, hh]))
+        deliver(group, lambda t: prod.at[0, t, hh], out_ref.at[:, y, z, hh, c], who)
 
     def plane_near(group, hh):
         if group == 0:
@@ -263,21 +271,22 @@
             split(slice(4, 8))
         own_plane(group, hh, far_rows, FAR)
         if group == 0:
-            row_ids = lax.broadcasted_iota(jnp.int32, (OWN, WIDTH), 0) + xl * OWN
-            col_ids = lax.broadcasted_iota(jnp.int32, (OWN, WIDTH), 1)
+            row_ids = lax.broadcasted_iota(jnp.int32, (TILES, 8, WIDTH), 0) * 8 + xl * OWN
+            row_ids += lax.broadcasted_iota(jnp.int32, (TILES, 8, WIDTH), 1)
+            col_ids = lax.broadcasted_iota(jnp.int32, (TILES, 8, WIDTH), 2)
             factor = jnp.where(row_ids == col_ids, jnp.float32(1.0 + damping), jnp.float32(1.0))
-            out_ref[y, z, hh, c] = prod[0, hh, mine, :] * factor
+            out_ref[:, y, z, hh, c] = prod[0, mine, hh] * factor
         else:
-            out_ref[y, z, hh, c] = prod[0, hh, mine, :]
+            out_ref[:, y, z, hh, c] = prod[0, mine, hh]
 
     def multiply(d):
         unit, zz = UNITS.index(d) + 1, origin(d)
         value = product(pl.ds(0, 8 * OWN), jnp.concatenate([cols[zz, 0], cols[zz, 1]], axis=1))
-        prod[unit, 0] = value[:, :WIDTH]
-        prod[unit, 1] = value[:, WIDTH:]
-        deliver(unit, lambda r: prod.at[unit, :, r, :], out_ref.at[y, zz, :, c], NEAR + FAR)
-        out_ref[y, zz, 0, c] = prod[unit, 0, mine, :]
-        out_ref[y, zz, 1, c] = prod[unit, 1, mine, :]
+        prod[unit, :, 0] = tiles_of(value[:, :WIDTH])
+        prod[unit, :, 1] = tiles_of(value[:, WIDTH:])
+        deliver(unit, lambda t: prod.at[unit, t], out_ref.at[:, y, zz, :, c], NEAR + FAR)
+        out_ref[:, y, zz, 0, c] = prod[unit, mine, 0]
+        out_ref[:, y, zz, 1, c] = prod[unit, mine, 1]
 
     def ring_start(dx, part):
         send(part, part, zl_s.at[0, dx], zl_r.at[0, dx], up)
@@ -353,10 +362,10 @@
         index = dy * 2 + dc - 1
         yy, cc = (y + dy * way + NY) % NY, (c + dc) % NC
         for group, hh in ((0, xh), (8, 1 - xh)):
-            arrived(out_ref.at[yy, z, hh, cc], out_r.at[group, index], out_s.at[group, index])
+            arrived(out_ref.at[:, yy, z, hh, cc], out_r.at[group, index], out_s.at[group, index])
         for unit, d in enumerate(UNITS):
             zz = (z + d * (1 - 2 * cc) + NZ) % NZ
-            arrived(out_ref.at[yy, zz, :, cc], out_r.at[unit + 1, index], out_s.at[unit + 1, index])
+            arrived(out_ref.at[:, yy, zz, :, cc], out_r.at[unit + 1, index], out_s.at[unit + 1, index])
     for copy in sends:
         copy.wait_send()
 
@@ -366,7 +375,7 @@
     tiles = pl.pallas_call(
         kernel,
         name="gather_multiply_scatter",
-        out_shape=jax.ShapeDtypeStruct((NY, NZ, 2, NC, OWN, WIDTH), jnp.float32),
+        out_shape=jax.ShapeDtypeStruct((TILES, NY, NZ, 2, NC, 8, WIDTH), jnp.float32),
         in_specs=[pl.BlockSpec(memory_space=pltpu.HBM)],
         out_specs=pl.BlockSpec(memory_space=pltpu.VMEM),
         scratch_shapes=[
@@ -376,7 +385,7 @@
             pltpu.VMEM((NY * NC * OWN, 2 * DEPTH), jnp.bfloat16),
             pltpu.VMEM((NY * NC * OWN, 2 * DEPTH), jnp.bfloat16),
             pltpu.VMEM((NZ, 2, 2 * DEPTH, WIDTH), jnp.float32),
-            pltpu.VMEM((NZ, 2, NY * NC * OWN, WIDTH), jnp.float32),
+            pltpu.VMEM((NZ, NY * NC * TILES, 2, 8, WIDTH), jnp.float32),
             dma,
             dma((1,)),
             dma((1,)),
@@ -400,9 +409,9 @@
         compiler_params=pltpu.CompilerParams(
             collective_id=0, has_side_effects=True, vmem_limit_bytes=48 * 2**20
         ),
-    )(jacobian)
-    tiles = tiles.reshape(NY * NZ * 2 * NC, OWN, WIDTH)
-    return jnp.transpose(tiles, (1, 0, 2)).reshape(OWN, NY * NZ * 2 * NC * WIDTH)
+    )(pltpu.with_memory_space_constraint(jacobian, pltpu.HBM))
+    tiles = tiles.reshape(TILES, NY * NZ * 2 * NC, 8, WIDTH)
+    return jnp.transpose(tiles, (0, 2, 1, 3)).reshape(OWN, NY * NZ * 2 * NC * WIDTH)
 
 
 def solution(mesh):

time: 75.8 us -> 74.3 us (0.980)
  local copies, waits for them, and re-layouts: 3.21 us -> 2.02 us
    reshape x1 -> x0, local copies, waits for them, and re-layouts: 2.28 us -> none  [per_device(): jnp.transpose(tiles, (1, 0, 2)).reshape(OWN, NY * NZ * 2 * NC * WIDTH)]
    unnamed x2 -> x1, local copies, waits for them, and re-layouts: 0.93 us -> 2.02 us
where the time goes in v4:
time: 74.3 us; the launch traced here: 74.2 us
  Pallas kernels  72.1 us (97%)
  local copies, waits for them, and re-layouts  2.02 us (3%)
    pallas_call x1, Pallas kernels, per_device(): pl.pallas_call(kernel, name='gather_multiply_scatter', out_shape=jax.Shap...  72.1 us
    unnamed x1, local copies, waits for them, and re-layouts  2.02 us

profile of v4, /device:TPU:1, one launch (start us, length us, event | category | flops | bytes accessed | tf_op | source)
XLA Modules:
  0.0 74.2 jit_solution(14933379950632878783)
XLA Ops:
  0.0 72.1 %gather_multiply_scatter.1 = f32[8,4,8,2,2,8,128]{6,5,4,3,2,1,0:T(8,128)S(1)} custom-call(f32[384,128]{1,0:T(8,128)} %a_ref.1), custom_call_target="tpu_custom_call" | custom-call | tf_op jit(solution)/shard_map/gather_multiply_scatter/pallas_call | solution.py:375
  72.1 2.0 %copy.3 = f32[64,16384]{1,0:T(8,128)} copy(f32[64,16384]{1,0:T(8,128)S(1)} %bitcast.5) | data formatting | bytes 8388608

commit v5 on v4

--- a/solution.py
+++ b/solution.py
@@ -16,6 +16,7 @@
 SLOT = {(1, 0): 0, (3, 0): 1, (1, 1): 2, (3, 1): 3, (2, 0): 4, (2, 1): 5, (0, 0): 6, (0, 1): 7}
 NEAR, FAR = ((1, 0), (3, 0), (1, 1), (3, 1)), ((2, 0), (2, 1), (0, 1))
 UNITS = (-1, 1, -2, 2, -3, 3, -4)
+MIRRORED = (-1, 1)
 DIRECT = (-1, 1, -2, 2)
 ORDER = (
     ("swap",),
@@ -94,6 +95,8 @@
     ("spread", 3, 2),
     ("multiply", 3),
     ("spread", -4, 2),
+    ("mirror", -1),
+    ("mirror", 1),
     ("multiply", -4),
 )
 
@@ -127,6 +130,10 @@
     xb_r,
     out_s,
     out_r,
+    turned_out,
+    turned_in,
+    mirror_s,
+    mirror_r,
 ):
     loop, xl = lax.axis_index("loop"), lax.axis_index("grp")
     c = loop % 2
@@ -177,6 +184,7 @@
     barrier = pltpu.get_barrier_semaphore()
     greeted = [device(dx=d) for d in (1, 2, 3)] + [device(dz=1), device(dz=-1), device(dc=1)]
     greeted += [device(dy=d, dc=e) for d in (1, 2, 3) for e in (0, 1)]
+    greeted += [(device(dz=d)[0], 1 - xl) for d in (1, -1)]
     for who in greeted:
         pl.semaphore_signal(barrier, inc=1, device_id=who, device_id_type=MESH)
     load.wait()
@@ -279,12 +287,34 @@
         else:
             out_ref[:, y, z, hh, c] = prod[0, mine, hh]
 
+    def mirror_send(d):
+        k, (there, _) = MIRRORED.index(d), device(dz=d)
+        for far, xx in ((0, xl), (1, 1 - xl)):
+            src = turned_out.at[k, pl.ds(pl.multiple_of(xx * OWN, 8), OWN), :]
+            send(src, turned_in.at[k, xl], mirror_s.at[k, far], mirror_r.at[k, far], (there, xx))
+
+    def mirror_arrived(d):
+        k, zz = MIRRORED.index(d), origin(-d)
+        for far, xx in ((0, xl), (1, 1 - xl)):
+            arrived(turned_in.at[k, xx], mirror_r.at[k, far], mirror_s.at[k, far])
+        for (dy, dc), slot in SLOT.items():
+            if dy:
+                part = slice(slot * OWN, (slot + 1) * OWN)
+                strip = jnp.concatenate([turned_in[k, 0][:, part], turned_in[k, 1][:, part]], axis=1)
+                out_ref[:, (y + dy * way + NY) % NY, zz, xh, (c + dc) % NC] = tiles_of(strip)
+
     def multiply(d):
         unit, zz = UNITS.index(d) + 1, origin(d)
         value = product(pl.ds(0, 8 * OWN), jnp.concatenate([cols[zz, 0], cols[zz, 1]], axis=1))
         prod[unit, :, 0] = tiles_of(value[:, :WIDTH])
         prod[unit, :, 1] = tiles_of(value[:, WIDTH:])
-        deliver(unit, lambda t: prod.at[unit, t], out_ref.at[:, y, zz, :, c], NEAR + FAR)
+        if d in MIRRORED:
+            deliver(unit, lambda t: prod.at[unit, t, 1 - xh], out_ref.at[:, y, zz, 1 - xh, c], NEAR + FAR[:2])
+            deliver(unit, lambda t: prod.at[unit, t], out_ref.at[:, y, zz, :, c], FAR[2:])
+            turned_out[MIRRORED.index(d)] = prod[unit, : 6 * TILES, xh].reshape(6 * OWN, WIDTH).T
+            mirror_send(d)
+        else:
+            deliver(unit, lambda t: prod.at[unit, t], out_ref.at[:, y, zz, :, c], NEAR + FAR)
         out_ref[:, y, zz, 0, c] = prod[unit, mine, 0]
         out_ref[:, y, zz, 1, c] = prod[unit, mine, 1]
 
@@ -351,6 +381,8 @@
                 spread(-at[0] if kind == "up" else at[0])
         elif kind == "spread":
             spread_came(at[0], at[1])
+        elif kind == "mirror":
+            mirror_arrived(at[0])
         elif kind == "near":
             plane_near(at[0], xh if at[0] == 0 else 1 - xh)
         elif kind == "far":
@@ -365,7 +397,8 @@
             arrived(out_ref.at[:, yy, z, hh, cc], out_r.at[group, index], out_s.at[group, index])
         for unit, d in enumerate(UNITS):
             zz = (z + d * (1 - 2 * cc) + NZ) % NZ
-            arrived(out_ref.at[:, yy, zz, :, cc], out_r.at[unit + 1, index], out_s.at[unit + 1, index])
+            part = out_ref.at[:, yy, zz, 1 - xh, cc] if dy and d in MIRRORED else out_ref.at[:, yy, zz, :, cc]
+            arrived(part, out_r.at[unit + 1, index], out_s.at[unit + 1, index])
     for copy in sends:
         copy.wait_send()
 
@@ -405,6 +438,10 @@
             dma((7, 3)),
             dma((9, 7)),
             dma((9, 7)),
+            pltpu.VMEM((len(MIRRORED), WIDTH, 6 * OWN), jnp.float32),
+            pltpu.VMEM((len(MIRRORED), 2, OWN, 6 * OWN), jnp.float32),
+            dma((len(MIRRORED), 2)),
+            dma((len(MIRRORED), 2)),
         ],
         compiler_params=pltpu.CompilerParams(
             collective_id=0, has_side_effects=True, vmem_limit_bytes=48 * 2**20

time: 74.3 us -> 74.9 us (level)
  no operation moved by 1% of the time
where the time goes in v5:
time: 74.9 us; the launch traced here: 74.8 us
  Pallas kernels  72.8 us (97%)
  local copies, waits for them, and re-layouts  2.02 us (3%)
    pallas_call x1, Pallas kernels, per_device(): pl.pallas_call(kernel, name='gather_multiply_scatter', out_shape=jax.Shap...  72.8 us
    unnamed x1, local copies, waits for them, and re-layouts  2.02 us

profile of v5, /device:TPU:1, one launch (start us, length us, event | category | flops | bytes accessed | tf_op | source)
XLA Modules:
  0.0 74.8 jit_solution(6433084606162695483)
XLA Ops:
  0.0 72.8 %gather_multiply_scatter.1 = f32[8,4,8,2,2,8,128]{6,5,4,3,2,1,0:T(8,128)S(1)} custom-call(f32[384,128]{1,0:T(8,128)} %a_ref.1), custom_call_target="tpu_custom_call" | custom-call | tf_op jit(solution)/shard_map/gather_multiply_scatter/pallas_call | solution.py:408
  72.8 2.0 %copy.3 = f32[64,16384]{1,0:T(8,128)} copy(f32[64,16384]{1,0:T(8,128)S(1)} %bitcast.5) | data formatting | bytes 8388608

commit v6 on v5

--- a/solution.py
+++ b/solution.py
@@ -17,7 +17,7 @@
 NEAR, FAR = ((1, 0), (3, 0), (1, 1), (3, 1)), ((2, 0), (2, 1), (0, 1))
 UNITS = (-1, 1, -2, 2, -3, 3, -4)
 MIRRORED = (-1, 1)
-DIRECT = (-1, 1, -2, 2)
+DIRECT = (-1, 1, -2, 2, -3, 3)
 ORDER = (
     ("swap",),
     ("rows", 0, 3),
@@ -81,23 +81,25 @@
     ("up", 3, "beyond"),
     ("spread", -3, 1),
     ("down", 3, "beyond"),
-    ("spread", 3, 3),
     ("up", 3, "opposite"),
-    ("spread", 3, 1),
     ("down", 3, "opposite"),
     ("spread", -3, 2),
     ("multiply", -3),
+    ("spread", 3, 3),
     ("up", 4, "across"),
-    ("spread", -4, 3),
+    ("spread", 3, 1),
     ("up", 4, "beyond"),
     ("up", 4, "opposite"),
-    ("spread", -4, 1),
     ("spread", 3, 2),
     ("multiply", 3),
+    ("mirror_send", -1),
+    ("mirror_send", 1),
+    ("spread", -4, 3),
+    ("spread", -4, 1),
     ("spread", -4, 2),
+    ("multiply", -4),
     ("mirror", -1),
     ("mirror", 1),
-    ("multiply", -4),
 )
 
 
@@ -289,6 +291,7 @@
 
     def mirror_send(d):
         k, (there, _) = MIRRORED.index(d), device(dz=d)
+        turned_out[k] = prod[UNITS.index(d) + 1, : 6 * TILES, xh].reshape(6 * OWN, WIDTH).T
         for far, xx in ((0, xl), (1, 1 - xl)):
             src = turned_out.at[k, pl.ds(pl.multiple_of(xx * OWN, 8), OWN), :]
             send(src, turned_in.at[k, xl], mirror_s.at[k, far], mirror_r.at[k, far], (there, xx))
@@ -311,8 +314,6 @@
         if d in MIRRORED:
             deliver(unit, lambda t: prod.at[unit, t, 1 - xh], out_ref.at[:, y, zz, 1 - xh, c], NEAR + FAR[:2])
             deliver(unit, lambda t: prod.at[unit, t], out_ref.at[:, y, zz, :, c], FAR[2:])
-            turned_out[MIRRORED.index(d)] = prod[unit, : 6 * TILES, xh].reshape(6 * OWN, WIDTH).T
-            mirror_send(d)
         else:
             deliver(unit, lambda t: prod.at[unit, t], out_ref.at[:, y, zz, :, c], NEAR + FAR)
         out_ref[:, y, zz, 0, c] = prod[unit, mine, 0]
@@ -381,6 +382,8 @@
                 spread(-at[0] if kind == "up" else at[0])
         elif kind == "spread":
             spread_came(at[0], at[1])
+        elif kind == "mirror_send":
+            mirror_send(at[0])
         elif kind == "mirror":
             mirror_arrived(at[0])
         elif kind == "near":
@@ -390,16 +393,22 @@
         else:
             multiply(at[0])
 
-    for dy, dc in NEAR + FAR:
-        index = dy * 2 + dc - 1
-        yy, cc = (y + dy * way + NY) % NY, (c + dc) % NC
-        for group, hh in ((0, xh), (8, 1 - xh)):
-            arrived(out_ref.at[:, yy, z, hh, cc], out_r.at[group, index], out_s.at[group, index])
-        for unit, d in enumerate(UNITS):
+    last = len(NEAR + FAR)
+    for copy in sends[:-last]:
+        copy.wait_send()
+    for group, d in ((0, 0), (8, 0), *((unit + 1, d) for unit, d in enumerate(UNITS))):
+        for dy, dc in NEAR + FAR:
+            index = dy * 2 + dc - 1
+            yy, cc = (y + dy * way + NY) % NY, (c + dc) % NC
             zz = (z + d * (1 - 2 * cc) + NZ) % NZ
-            part = out_ref.at[:, yy, zz, 1 - xh, cc] if dy and d in MIRRORED else out_ref.at[:, yy, zz, :, cc]
-            arrived(part, out_r.at[unit + 1, index], out_s.at[unit + 1, index])
-    for copy in sends:
+            if d == 0:
+                part = out_ref.at[:, yy, z, xh if group == 0 else 1 - xh, cc]
+            elif dy and d in MIRRORED:
+                part = out_ref.at[:, yy, zz, 1 - xh, cc]
+            else:
+                part = out_ref.at[:, yy, zz, :, cc]
+            arrived(part, out_r.at[group, index], out_s.at[group, index])
+    for copy in sends[-last:]:
         copy.wait_send()
 
 

time: 74.9 us -> 73.3 us (0.979)
  Pallas kernels: 72.8 us -> 71.2 us
    pallas_call x1, Pallas kernels: 72.8 us -> 71.2 us  [per_device(): pl.pallas_call(kernel, name='gather_multiply_scatter', out_shape=jax.Shap...]
where the time goes in v6:
time: 73.3 us; the launch traced here: 73.2 us
  Pallas kernels  71.2 us (97%)
  local copies, waits for them, and re-layouts  2.02 us (3%)
    pallas_call x1, Pallas kernels, per_device(): pl.pallas_call(kernel, name='gather_multiply_scatter', out_shape=jax.Shap...  71.2 us
    unnamed x1, local copies, waits for them, and re-layouts  2.02 us

profile of v6, /device:TPU:1, one launch (start us, length us, event | category | flops | bytes accessed | tf_op | source)
XLA Modules:
  0.0 73.2 jit_solution(2558713332618980225)
XLA Ops:
  0.0 71.2 %gather_multiply_scatter.1 = f32[8,4,8,2,2,8,128]{6,5,4,3,2,1,0:T(8,128)S(1)} custom-call(f32[384,128]{1,0:T(8,128)} %a_ref.1), custom_call_target="tpu_custom_call" | custom-call | tf_op jit(solution)/shard_map/gather_multiply_scatter/pallas_call | solution.py:417
  71.2 2.0 %copy.3 = f32[64,16384]{1,0:T(8,128)} copy(f32[64,16384]{1,0:T(8,128)S(1)} %bitcast.5) | data formatting | bytes 8388608

commit v7 on v6

--- a/solution.py
+++ b/solution.py
@@ -205,7 +205,7 @@
     )
 
     def give_rows(part, lanes):
-        for to, there in ((1, 3), (-1, 1)):
+        for to, there in ((1, 3), (-1, 1), (2, 2)):
             send(
                 rows_f32.at[SLOT[0, 0], :, lanes],
                 rows_f32.at[SLOT[there, 0], :, lanes],
@@ -217,8 +217,6 @@
     def rows_arrived(part, lanes, dy):
         slot = rows_f32.at[SLOT[dy, 0], :, lanes]
         arrived(slot, row_r.at[part, dy - 1], row_s.at[part, dy - 1])
-        if dy == 3:
-            send(slot, rows_f32.at[SLOT[2, 0], :, lanes], row_s.at[part, 1], row_r.at[part, 1], device(dy=1))
 
     def pass_rows(dy):
         send(

time: 73.3 us -> 73.2 us (level)
  no operation moved by 1% of the time
where the time goes in v7:
time: 73.2 us; the launch traced here: 73.1 us
  Pallas kernels  71.1 us (97%)
  local copies, waits for them, and re-layouts  2.02 us (3%)
    pallas_call x1, Pallas kernels, per_device(): pl.pallas_call(kernel, name='gather_multiply_scatter', out_shape=jax.Shap...  71.1 us
    unnamed x1, local copies, waits for them, and re-layouts  2.02 us

profile of v7, /device:TPU:1, one launch (start us, length us, event | category | flops | bytes accessed | tf_op | source)
XLA Modules:
  0.0 73.1 jit_solution(12667055876489955165)
XLA Ops:
  0.0 71.1 %gather_multiply_scatter.1 = f32[8,4,8,2,2,8,128]{6,5,4,3,2,1,0:T(8,128)S(1)} custom-call(f32[384,128]{1,0:T(8,128)} %a_ref.1), custom_call_target="tpu_custom_call" | custom-call | tf_op jit(solution)/shard_map/gather_multiply_scatter/pallas_call | solution.py:415
  71.1 2.0 %copy.3 = f32[64,16384]{1,0:T(8,128)} copy(f32[64,16384]{1,0:T(8,128)S(1)} %bitcast.5) | data formatting | bytes 8388608

commit v8 on v7

--- a/solution.py
+++ b/solution.py
@@ -17,7 +17,7 @@
 NEAR, FAR = ((1, 0), (3, 0), (1, 1), (3, 1)), ((2, 0), (2, 1), (0, 1))
 UNITS = (-1, 1, -2, 2, -3, 3, -4)
 MIRRORED = (-1, 1)
-DIRECT = (-1, 1, -2, 2, -3, 3)
+DIRECT = (-1, 1, -2, 2, -3, 3, -4)
 ORDER = (
     ("swap",),
     ("rows", 0, 3),

time: 73.2 us -> 73.2 us (level)
  no operation moved by 1% of the time
where the time goes in v8:
time: 73.2 us; the launch traced here: 73.1 us
  Pallas kernels  71.1 us (97%)
  local copies, waits for them, and re-layouts  2.02 us (3%)
    pallas_call x1, Pallas kernels, per_device(): pl.pallas_call(kernel, name='gather_multiply_scatter', out_shape=jax.Shap...  71.1 us
    unnamed x1, local copies, waits for them, and re-layouts  2.02 us

profile of v8, /device:TPU:1, one launch (start us, length us, event | category | flops | bytes accessed | tf_op | source)
XLA Modules:
  0.0 73.1 jit_solution(3902947533402348315)
XLA Ops:
  0.0 71.1 %gather_multiply_scatter.1 = f32[8,4,8,2,2,8,128]{6,5,4,3,2,1,0:T(8,128)S(1)} custom-call(f32[384,128]{1,0:T(8,128)} %a_ref.1), custom_call_target="tpu_custom_call" | custom-call | tf_op jit(solution)/shard_map/gather_multiply_scatter/pallas_call | solution.py:415
  71.1 2.0 %copy.3 = f32[64,16384]{1,0:T(8,128)} copy(f32[64,16384]{1,0:T(8,128)S(1)} %bitcast.5) | data formatting | bytes 8388608

commit v9 on v7

--- a/solution.py
+++ b/solution.py
@@ -313,7 +313,7 @@
             deliver(unit, lambda t: prod.at[unit, t, 1 - xh], out_ref.at[:, y, zz, 1 - xh, c], NEAR + FAR[:2])
             deliver(unit, lambda t: prod.at[unit, t], out_ref.at[:, y, zz, :, c], FAR[2:])
         else:
-            deliver(unit, lambda t: prod.at[unit, t], out_ref.at[:, y, zz, :, c], NEAR + FAR)
+            deliver(unit, lambda t: prod.at[unit, t], out_ref.at[:, y, zz, :, c], FAR + NEAR)
         out_ref[:, y, zz, 0, c] = prod[unit, mine, 0]
         out_ref[:, y, zz, 1, c] = prod[unit, mine, 1]
 

time: 73.2 us -> 73.1 us (level)
  no operation moved by 1% of the time
where the time goes in v9:
time: 73.1 us; the launch traced here: 73 us
  Pallas kernels  71 us (97%)
  local copies, waits for them, and re-layouts  2.02 us (3%)
    pallas_call x1, Pallas kernels, per_device(): pl.pallas_call(kernel, name='gather_multiply_scatter', out_shape=jax.Shap...  71 us
    unnamed x1, local copies, waits for them, and re-layouts  2.02 us

profile of v9, /device:TPU:1, one launch (start us, length us, event | category | flops | bytes accessed | tf_op | source)
XLA Modules:
  0.0 73.0 jit_solution(6674143154419442626)
XLA Ops:
  0.0 71.0 %gather_multiply_scatter.1 = f32[8,4,8,2,2,8,128]{6,5,4,3,2,1,0:T(8,128)S(1)} custom-call(f32[384,128]{1,0:T(8,128)} %a_ref.1), custom_call_target="tpu_custom_call" | custom-call | tf_op jit(solution)/shard_map/gather_multiply_scatter/pallas_call | solution.py:415
  71.0 2.0 %copy.3 = f32[64,16384]{1,0:T(8,128)} copy(f32[64,16384]{1,0:T(8,128)S(1)} %bitcast.5) | data formatting | bytes 8388608
